TPU v7x, 128 devices: a whole 4x4x4 slice. The times are simulated.
128 devices in a mesh: room: 4 (over x_hi, core), geom: 32 (over z, x_lo, y).
Axes of the slice: x: 4 (x_hi: 2, x_lo: 2; x = x_hi * 2 + x_lo), y: 4, z: 4, core: 2. Of those that a mesh axis runs over, the one named last changes fastest.
Arguments:
- queries: bfloat16 [4, 4096, 512], P('room', 'geom'), may hold values from -6 to 6
- features: bfloat16 [4, 4096, 512], P('room', 'geom'), may hold values from -45 to 45
- visible: int32 [4, 32, 32], P('room', 'geom'), may hold values from 0 to 1, as said below
- cotangent: bfloat16 [4, 4096, 512], P('room', 'geom'), may hold values from -0.125 to 0.125
- w_query: bfloat16 [512, 512], replicated, may hold values from -0.25 to 0.25
- w_key: bfloat16 [512, 512], replicated, may hold values from -0.25 to 0.25
- w_value: bfloat16 [512, 512], replicated, may hold values from -0.25 to 0.25
- w_out: bfloat16 [512, 512], replicated, may hold values from -0.25 to 0.25
- w_up: bfloat16 [512, 1024], replicated, may hold values from -0.25 to 0.25
- w_down: bfloat16 [1024, 512], replicated, may hold values from -0.1875 to 0.1875
- gain_attn: float32 [512], replicated, may hold values from 0.25 to 1.75
- gain_mlp: float32 [512], replicated, may hold values from 0.25 to 1.75
Outputs:
- output: bfloat16 [4, 4096, 512], P('room', 'geom')
- grad_query_w: bfloat16 [512, 512], replicated
- grad_key_w: bfloat16 [512, 512], replicated
- grad_value_w: bfloat16 [512, 512], replicated
- grad_out_w: bfloat16 [512, 512], replicated
- grad_up_w: bfloat16 [512, 1024], replicated
- grad_down_w: bfloat16 [1024, 512], replicated
- grad_gain_attn: bfloat16 [512], replicated
- grad_gain_mlp: bfloat16 [512], replicated
Inputs may be any that keep to these rules, and one draw needn't show every extreme that they name: `visible`: every query block sees at least one key block.
All inputs are finite; a program needn't handle non-finite values.
Results may differ from a plain program's by a relative error of at most 0.017.
The roundings to bfloat16 on the way count: a program that leaves them out, or rounds other values in their place, can miss the bound.
Values may be sent and summed in bfloat16 or wider, within the bound.
No kernel may reach another device: no remote copies, remote signals or barrier semaphores. Data moves between devices by JAX's collectives and lax.ppermute only.
A program may use at most 128 MiB of HBM per device.

v0:
```python
import math
import jax
import jax.numpy as jnp
from jax import lax
from jax.sharding import PartitionSpec as P

HEADS = 4
BLK = 128
EPSILON = 1e-05
GELU_COEF = math.sqrt(2.0 / math.pi)


def normalize(inputs, gain):
    center = inputs - jnp.mean(inputs, axis=-1, keepdims=True)
    inverse = lax.rsqrt(jnp.mean(center * center, axis=-1, keepdims=True) + EPSILON)
    scaled = center * inverse
    return (scaled, inverse, scaled * gain)


def gelu_pair(inputs):
    inner = GELU_COEF * (inputs + 0.044715 * inputs * inputs * inputs)
    tangent = jnp.tanh(inner)
    value = 0.5 * inputs * (1.0 + tangent)
    slope = 0.5 * (1.0 + tangent) + 0.5 * inputs * (1.0 - tangent * tangent) * GELU_COEF * (
        1.0 + 3.0 * 0.044715 * inputs * inputs
    )
    return (value, slope)


def mult_nt(left, right):
    return lax.dot_general(
        left, right, (((1,), (1,)), ((), ())), preferred_element_type=jnp.float32
    )


def mult_tn(left, right):
    return lax.dot_general(
        left, right, (((0,), (0,)), ((), ())), preferred_element_type=jnp.float32
    )


def device_step(
    queries,
    visible,
    cotangent,
    key_rows,
    value_rows,
    w_query,
    w_out,
    w_up,
    w_down,
    gain_attn,
    gain_mlp,
):
    head_size = key_rows.shape[1] // HEADS
    factor = 1.0 / math.sqrt(head_size)
    allowed = jnp.repeat(jnp.repeat(visible > 0, BLK, axis=0), BLK, axis=1)
    inputs = queries.astype(jnp.float32)
    scaled_one, inverse_one, normed = normalize(inputs, gain_attn)
    normed_b = normed.astype(jnp.bfloat16)
    query_rows = jnp.dot(normed_b, w_query, preferred_element_type=jnp.float32).astype(jnp.bfloat16)
    contexts = []
    saved = []
    for head_index in range(HEADS):
        lower = head_index * head_size
        query_head = query_rows[:, lower : lower + head_size]
        key_head = key_rows[:, lower : lower + head_size]
        value_head = value_rows[:, lower : lower + head_size]
        scores = mult_nt(query_head, key_head) * factor
        scores = jnp.where(allowed, scores, -1e30)
        highest = jnp.max(scores, axis=-1, keepdims=True)
        expo = jnp.exp(scores - highest)
        attend = expo / jnp.sum(expo, axis=-1, keepdims=True)
        attend_b = attend.astype(jnp.bfloat16)
        contexts.append(
            jnp.dot(attend_b, value_head, preferred_element_type=jnp.float32).astype(jnp.bfloat16)
        )
        saved.append((attend, attend_b))
    context = jnp.concatenate(contexts, axis=1)
    mixed = inputs + jnp.dot(context, w_out, preferred_element_type=jnp.float32)
    scaled_two, inverse_two, normed_two = normalize(mixed, gain_mlp)
    normed_two_b = normed_two.astype(jnp.bfloat16)
    upper = jnp.dot(normed_two_b, w_up, preferred_element_type=jnp.float32)
    activated, slope = gelu_pair(upper)
    activated_b = activated.astype(jnp.bfloat16)
    output = (mixed + jnp.dot(activated_b, w_down, preferred_element_type=jnp.float32)).astype(
        jnp.bfloat16
    )
    grad_down = mult_tn(activated_b, cotangent)
    grad_activated = mult_nt(cotangent, w_down)
    grad_upper_b = (grad_activated * slope).astype(jnp.bfloat16)
    grad_up = mult_tn(normed_two_b, grad_upper_b)
    grad_normed_two = mult_nt(grad_upper_b, w_up)
    grad_gain_mlp = jnp.sum(grad_normed_two * scaled_two, axis=0)
    grad_scaled = grad_normed_two * gain_mlp
    mean_one = jnp.mean(grad_scaled, axis=-1, keepdims=True)
    mean_two = jnp.mean(grad_scaled * scaled_two, axis=-1, keepdims=True)
    grad_mixed = cotangent.astype(jnp.float32) + inverse_two * (
        grad_scaled - mean_one - scaled_two * mean_two
    )
    grad_mixed_b = grad_mixed.astype(jnp.bfloat16)
    grad_out = mult_tn(context, grad_mixed_b)
    grad_context = mult_nt(grad_mixed_b, w_out).astype(jnp.bfloat16)
    grad_queries = []
    grad_keys = []
    grad_values = []
    for head_index in range(HEADS):
        lower = head_index * head_size
        query_head = query_rows[:, lower : lower + head_size]
        key_head = key_rows[:, lower : lower + head_size]
        value_head = value_rows[:, lower : lower + head_size]
        attend, attend_b = saved[head_index]
        grad_head = grad_context[:, lower : lower + head_size]
        grad_attend = mult_nt(grad_head, value_head)
        grad_values.append(mult_tn(attend_b, grad_head))
        centre = jnp.sum(attend * grad_attend, axis=-1, keepdims=True)
        grad_scores = (attend * (grad_attend - centre) * factor).astype(jnp.bfloat16)
        grad_queries.append(jnp.dot(grad_scores, key_head, preferred_element_type=jnp.float32))
        grad_keys.append(mult_tn(grad_scores, query_head))
    grad_query_rows = jnp.concatenate(grad_queries, axis=1).astype(jnp.bfloat16)
    partial_keys = jnp.concatenate(grad_keys, axis=1).astype(jnp.bfloat16)
    partial_values = jnp.concatenate(grad_values, axis=1).astype(jnp.bfloat16)
    grad_query = mult_tn(normed_b, grad_query_rows)
    grad_normed = mult_nt(grad_query_rows, w_query)
    grad_gain_attn = jnp.sum(grad_normed * scaled_one, axis=0)
    grads = (grad_query, grad_out, grad_up, grad_down, grad_gain_attn, grad_gain_mlp)
    return (output, grads, partial_keys, partial_values)


def local(
    queries,
    features,
    visible,
    cotangent,
    w_query,
    w_key,
    w_value,
    w_out,
    w_up,
    w_down,
    gain_attn,
    gain_mlp,
):
    local_feat = features[0]
    local_keys = jnp.dot(local_feat, w_key, preferred_element_type=jnp.float32).astype(jnp.bfloat16)
    local_values = jnp.dot(local_feat, w_value, preferred_element_type=jnp.float32).astype(
        jnp.bfloat16
    )
    key_rows, value_rows = (
        lax.all_gather(local_keys, "geom", axis=0, tiled=True),
        lax.all_gather(local_values, "geom", axis=0, tiled=True),
    )
    output, grads, partial_keys, partial_values = device_step(
        queries[0],
        visible[0],
        cotangent[0],
        key_rows,
        value_rows,
        w_query,
        w_out,
        w_up,
        w_down,
        gain_attn,
        gain_mlp,
    )
    key_sum, value_sum = (
        lax.psum_scatter(partial_keys.astype(jnp.float32), "geom", scatter_dimension=0, tiled=True),
        lax.psum_scatter(
            partial_values.astype(jnp.float32), "geom", scatter_dimension=0, tiled=True
        ),
    )
    feat_float = local_feat.astype(jnp.float32)
    grad_key = lax.dot_general(
        feat_float,
        key_sum,
        (((0,), (0,)), ((), ())),
        precision=lax.Precision.HIGHEST,
        preferred_element_type=jnp.float32,
    )
    grad_value = lax.dot_general(
        feat_float,
        value_sum,
        (((0,), (0,)), ((), ())),
        precision=lax.Precision.HIGHEST,
        preferred_element_type=jnp.float32,
    )
    grad_query, grad_out, grad_up, grad_down, grad_gain_attn, grad_gain_mlp = grads
    totals = lax.psum(
        (
            grad_query,
            grad_key,
            grad_value,
            grad_out,
            grad_up,
            grad_down,
            grad_gain_attn,
            grad_gain_mlp,
        ),
        ("room", "geom"),
    )
    summed = [piece.astype(jnp.bfloat16) for piece in totals]
    return (
        output[None],
        summed[0],
        summed[1],
        summed[2],
        summed[3],
        summed[4],
        summed[5],
        summed[6],
        summed[7],
    )


def solution(mesh):
    placed = (
        P("room", "geom", None),
        P("room", "geom", None),
        P("room", "geom", None),
        P("room", "geom", None),
        P(),
        P(),
        P(),
        P(),
        P(),
        P(),
        P(),
        P(),
    )
    return jax.shard_map(
        local,
        mesh=mesh,
        in_specs=placed,
        out_specs=(P("room", "geom", None), P(), P(), P(), P(), P(), P(), P(), P()),
        check_vma=False,
    )
```

profile of v0, /device:TPU:0, one launch (start us, length us, event | category | flops | bytes accessed | tf_op | source)
XLA Modules:
  0.0 832.1 jit_solution(216690923784676051)
XLA Ops:
  7.3 2.1 convolution_convert_fusion.10
  9.5 2.0 convolution_convert_fusion.9
  11.5 1.0 convert_reduce_fusion
  12.6 1.1 fusion.54
  14.1 156.3 %all-gather.3.cloned.1.call-done = bf16[4096,512]{1,0:T(8,128)(2,1)} async-done(((bf16[128,512]{1,0:T(8,128)(2,1)}), bf16[4096,512]{1,0:T(8,128)(2,1)}) %all-gather.3.cloned.1.call-update) | async-done | bytes 4194320 | tf_op jit(solution)/shard_map/all_gather | solution.py:150
  170.4 1.9 fusion.99
  172.3 1.4 copy-done.8
  173.7 0.4 fusion.5
  174.2 0.6 fusion.98
  174.7 1.3 copy-done.5
  176.0 0.4 fusion.7
  176.4 0.5 fusion.97
  177.0 0.4 fusion.9
  177.5 0.5 fusion.96
  178.3 0.4 fusion.11
  178.8 151.2 %all-gather.5.cloned.1.call-done = bf16[4096,512]{1,0:T(8,128)(2,1)} async-done(((bf16[128,512]{1,0:T(8,128)(2,1)}), bf16[4096,512]{1,0:T(8,128)(2,1)}) %all-gather.5.cloned.1.call-update) | async-done | bytes 4194320 | tf_op jit(solution)/shard_map/all_gather | solution.py:151
  329.9 2.7 convolution_convert_fusion.19
  332.7 1.0 copy-done.78
  333.7 0.7 convolution_convert_fusion.18
  334.5 0.8 copy-done.3
  335.3 0.7 convolution_convert_fusion.17
  336.1 0.7 convolution_convert_fusion.16
  338.5 0.6 fusion.12
  339.1 1.1 multiply_reduce_fusion.4
  340.7 0.6 convolution_convert_fusion.2
  341.4 1.0 copy-done.9
  342.4 0.6 convolution_convert_fusion.3
  343.0 0.6 convolution_convert_fusion.1
  343.7 0.6 convolution_convert_fusion
  344.3 3.6 maximum_convert_fusion.1
  348.6 2.7 multiply_reduce_fusion.3
  351.3 0.7 multiply_convert_fusion.3
  352.2 0.5 convolution_convert_fusion.7
  352.7 0.9 copy-done.79
  353.7 0.9 copy-done.7
  354.5 0.7 multiply_reduce_fusion.2
  355.2 0.7 multiply_convert_fusion.2
  356.0 0.5 convolution_convert_fusion.6
  356.4 1.5 copy-done.4
  357.9 0.7 multiply_reduce_fusion.1
  358.6 0.7 multiply_convert_fusion.1
  359.4 0.5 convolution_convert_fusion.5
  360.1 0.7 multiply_reduce_fusion
  360.8 0.7 multiply_convert_fusion
  361.5 1.0 copy-done.17
  362.4 0.5 convolution_convert_fusion.4
  362.9 3.9 maximum_convert_fusion
  366.8 1.9 convolution_convert_fusion.15
  368.8 2.1 convolution_convert_fusion.14
  370.9 0.6 convolution_convert_fusion.13
  371.5 0.6 convolution_convert_fusion.12
  372.1 0.9 fusion.14
  373.0 0.5 fusion.86
  373.6 1.3 fusion.79
  374.9 1.4 fusion.78
  376.3 1.9 fusion.55
  378.1 1.0 fusion.15
  379.2 147.8 %reduce-scatter.5.cloned.1.call-done = f32[128,512]{1,0:T(8,128)} async-done(((f32[4096,512]{1,0:T(8,128)}), f32[128,512]{1,0:T(8,128)}) %reduce-scatter.5.cloned.1.call-update) | async-done | bytes 262160 | tf_op jit(solution)/shard_map/reduce_scatter | solution.py:168
  526.9 2.5 convolution_bitcast_fusion
  529.5 174.9 %reduce-scatter.3.cloned.1.call-done = f32[128,512]{1,0:T(8,128)} async-done(((f32[4096,512]{1,0:T(8,128)}), f32[128,512]{1,0:T(8,128)}) %reduce-scatter.3.cloned.1.call-update) | async-done | bytes 262160 | tf_op jit(solution)/shard_map/reduce_scatter | solution.py:167
  704.4 2.6 convolution_bitcast_fusion.1
  707.0 114.5 %all-reduce.2 = (bf16[512,512]{1,0:T(8,128)(2,1)}, bf16[512,512]{0,1:T(8,128)(2,1)}, bf16[512,512]{0,1:T(8,128)(2,1)}, bf16[512,512]{1,0:T(8,128)(2,1)}, bf16[51...) all-reduce(f32[512,512]{1,0:T(8,128)} %fusion.78, ...), channel_id=1, replica_groups=mesh['room'=4,'geom'=32] {'room','geom'}, use_global_device_ids=true, to_apply=%region_18.19 | all-reduce | flops 2098176 | bytes 12589056 | tf_op jit(solution)/shard_map/psum | solution.py:188
  821.4 2.0 copy.21
  823.5 2.0 copy.22
  (178 shorter events, 4.3 us)
Async XLA Ops:
  7.2 330.5 %copy-start = (bf16[512,1024]{1,0:T(8,128)(2,1)S(1)}, bf16[512,1024]{1,0:T(8,128)(2,1)}, u32[]{:S(2)}) copy-start(bf16[512,1024]{1,0:T(8,128)(2,1)} %param.20) | copy-start | bytes 3145732
  7.2 6.6 copy-start.19
  7.2 6.5 copy-start.82
  7.2 6.6 copy-start.30
  7.2 6.6 copy-start.45
  7.2 163.2 %all-gather.3.cloned.1.call-start = ((), (), s32[]{:S(2)}) async-start(), calls=%async_computation.2 | async-start | bytes 4325376 | tf_op jit(solution)/shard_map/all_gather | solution.py:150
  9.4 320.5 %all-gather.5.cloned.1.call-start = ((), (), s32[]{:S(2)}) async-start(), calls=%async_computation.3 | async-start | bytes 4325376 | tf_op jit(solution)/shard_map/all_gather | solution.py:151
  11.5 515.4 %reduce-scatter.5.cloned.1.call-start = ((), (), s32[]{:S(2)}) async-start(), calls=%async_computation.5 | async-start | bytes 8650752 | tf_op jit(solution)/shard_map/reduce_scatter | solution.py:168
  12.6 161.6 %copy-start.47 = (f32[128]{0:T(128)}, f32[128]{0:T(128)S(1)}, u32[]{:S(2)}) copy-start(f32[128]{0:T(128)S(1)} %broadcast_multiply_fusion.3) | copy-start | bytes 1540
  13.7 160.4 %copy-start.62 = (f32[128]{0:T(128)}, f32[128]{0:T(128)S(1)}, u32[]{:S(2)}) copy-start(f32[128]{0:T(128)S(1)} %add_rsqrt_fusion.1) | copy-start | bytes 1540
  14.1 163.4 %copy-start.24 = (bf16[128,512]{1,0:T(8,128)(2,1)}, bf16[128,512]{1,0:T(8,128)(2,1)S(1)}, u32[]{:S(2)}) copy-start(bf16[128,512]{1,0:T(8,128)(2,1)S(1)} %convolution_convert_fusion.11) | copy-start | bytes 393220
  170.4 3.7 copy-start.11
  172.3 157.6 %copy-start.58 = (f32[128]{0:T(128)}, f32[128]{0:T(128)S(1)}, u32[]{:S(2)}) copy-start(f32[128]{0:T(128)S(1)} %get-tuple-element.35) | copy-start | bytes 1540
  174.1 155.8 %copy-start.73 = (f32[128]{0:T(128)}, f32[128]{0:T(128)S(1)}, u32[]{:S(2)}) copy-start(f32[128]{0:T(128)S(1)} %fusion.5) | copy-start | bytes 1540
  174.7 157.9 %copy-start.55 = (f32[128]{0:T(128)}, f32[128]{0:T(128)S(1)}, u32[]{:S(2)}) copy-start(f32[128]{0:T(128)S(1)} %get-tuple-element.33) | copy-start | bytes 1540
  176.4 156.2 %copy-start.70 = (f32[128]{0:T(128)}, f32[128]{0:T(128)S(1)}, u32[]{:S(2)}) copy-start(f32[128]{0:T(128)S(1)} %fusion.7) | copy-start | bytes 1540
  177.0 157.5 %copy-start.52 = (f32[128]{0:T(128)}, f32[128]{0:T(128)S(1)}, u32[]{:S(2)}) copy-start(f32[128]{0:T(128)S(1)} %get-tuple-element.31) | copy-start | bytes 1540
  177.5 157.0 %copy-start.67 = (f32[128]{0:T(128)}, f32[128]{0:T(128)S(1)}, u32[]{:S(2)}) copy-start(f32[128]{0:T(128)S(1)} %fusion.9) | copy-start | bytes 1540
  178.3 157.7 %copy-start.49 = (f32[128]{0:T(128)}, f32[128]{0:T(128)S(1)}, u32[]{:S(2)}) copy-start(f32[128]{0:T(128)S(1)} %get-tuple-element.29) | copy-start | bytes 1540
  178.7 157.3 %copy-start.64 = (f32[128]{0:T(128)}, f32[128]{0:T(128)S(1)}, u32[]{:S(2)}) copy-start(f32[128]{0:T(128)S(1)} %fusion.11) | copy-start | bytes 1540
  329.9 2.7 copy-start.6
  329.9 3.8 copy-start.78
  333.7 3.1 copy-start.36
  333.7 1.6 copy-start.3
  335.3 1.5 copy-start.38
  336.1 1.6 copy-start.44
  337.1 1.9 copy-start.42
  338.5 1.7 copy-start.21
  339.1 1.6 copy-start.56
  339.1 1.6 copy-start.71
  340.7 3.0 copy-start.34
  340.7 1.6 copy-start.9
  340.7 1.6 copy-start.59
  340.7 1.6 copy-start.74
  347.9 356.5 %reduce-scatter.3.cloned.1.call-start = ((), (), s32[]{:S(2)}) async-start(), calls=%async_computation.4 | async-start | bytes 8650752 | tf_op jit(solution)/shard_map/reduce_scatter | solution.py:167
  348.5 2.7 copy-start.10
  348.5 2.8 copy-start.61
  348.5 2.8 copy-start.76
  351.3 2.3 copy-start.79
  352.2 2.3 copy-start.7
  352.2 2.3 copy-start.57
  352.2 2.3 copy-start.72
  355.9 2.7 copy-start.13
  355.9 2.0 copy-start.4
  355.9 2.0 copy-start.54
  356.0 2.0 copy-start.69
  359.3 1.4 copy-start.15
  366.8 2.0 copy-start.14
  366.8 4.0 copy-start.16
  366.8 4.0 copy-start.12
  368.8 2.7 copy-start.18
  371.5 1.6 copy-start.29
  372.1 1.5 copy-start.27
  372.1 1.5 copy-start.37
  372.1 1.5 copy-start.39
  372.1 1.5 copy-start.41
  372.1 1.5 copy-start.43
  373.0 3.3 copy-start.22
  373.0 3.3 copy-start.33
  374.9 3.3 copy-start.81
  376.3 150.7 %copy-start.23 = (bf16[1,128,512]{2,1,0:T(8,128)(2,1)S(1)}, bf16[1,128,512]{2,1,0:T(8,128)(2,1)}, u32[]{:S(2)}) copy-start(bf16[1,128,512]{2,1,0:T(8,128)(2,1)} %param.13) | copy-start | bytes 393220
  378.1 328.8 %copy-start.46 = (f32[512]{0:T(512)S(1)}, f32[512]{0:T(512)}, u32[]{:S(2)}) copy-start(f32[512]{0:T(512)} %get-tuple-element.18) | copy-start | bytes 6148
  378.1 328.8 %copy-start.77 = (f32[512]{0:T(512)S(1)}, f32[512]{0:T(512)}, u32[]{:S(2)}) copy-start(f32[512]{0:T(512)} %fusion.14) | copy-start | bytes 6148
  707.0 118.6 %copy-start.1 = (bf16[512,1024]{1,0:T(8,128)(2,1)S(1)}, bf16[512,1024]{1,0:T(8,128)(2,1)}, u32[]{:S(2)}) copy-start(bf16[512,1024]{1,0:T(8,128)(2,1)} %param.20) | copy-start | bytes 3145732
  (23 other events, 22.6 us)
Sparse Core Ops, SparseCore 0:
  10.3 160.0 all-gather.2
  172.6 157.2 all-gather.4
  348.0 178.8 reduce-scatter.4
  529.2 175.1 reduce-scatter.2
where the time goes:
time: 833 us; the launch traced here: 832 us
  waiting for transfers between devices  630 us (76%)
  blocking collectives  114 us (14%)
  matrix products  41.7 us (5%)
  local copies, waits for them, and re-layouts  16 us (2%)
  between operations  14.7 us (2%)
  other arithmetic  14.5 us (2%)
    reduce_scatter x1, waiting for transfers between devices, local(): lax.psum_scatter(partial_keys.astype(jnp.float32), 'geom', scatter_dimens...  175 us
    all_gather x1, waiting for transfers between devices, local(): lax.all_gather(local_keys, 'geom', axis=0, tiled=True)  156 us
    all_gather x1, waiting for transfers between devices, local(): lax.all_gather(local_values, 'geom', axis=0, tiled=True)  151 us
    reduce_scatter x1, waiting for transfers between devices, local(): lax.psum_scatter(partial_values.astype(jnp.float32), 'geom', scatter_dime...  148 us
    psum x1, blocking collectives, local(): lax.psum((grad_query, grad_key, grad_value, grad_out, grad_up, grad_down,...  114 us
  transfers between devices with their start and end apart: 4, of which 4 were waited for; matrix products, arithmetic and copies ran while one was open for 5% of the time, Pallas kernels for 0%

commit v1 on v0

--- a/solution.py
+++ b/solution.py
@@ -147,7 +147,9 @@
         jnp.bfloat16
     )
     key_rows, value_rows = (
-        lax.all_gather(local_keys, "geom", axis=0, tiled=True),
+        jnp.concatenate(
+            lax.all_to_all(jnp.stack([local_keys] * lax.axis_size("geom")), "geom", 0, 0), axis=0
+        ),
         lax.all_gather(local_values, "geom", axis=0, tiled=True),
     )
     output, grads, partial_keys, partial_values = device_step(

time: 833 us -> 703 us (0.84)
  waiting for transfers between devices: 630 us -> 485 us
  starting transfers between devices: 0.34 us -> 9.92 us
    all_gather x1 -> x0, waiting for transfers between devices: 156 us -> none  [local(): lax.all_gather(local_keys, 'geom', axis=0, tiled=True)]
    all_to_all x0 -> x1, waiting for transfers between devices: none -> 64.3 us  [local(): lax.all_to_all(jnp.stack([local_keys] * lax.axis_size('geom')), 'geom', 0...]
    all_gather x1, waiting for transfers between devices: 151 us -> 101 us  [local(): lax.all_gather(local_values, 'geom', axis=0, tiled=True)]
    all_to_all x0 -> x1, starting transfers between devices: none -> 9.62 us  [local(): lax.all_to_all(jnp.stack([local_keys] * lax.axis_size('geom')), 'geom', 0...]
  transfers between devices with their start and end apart: 4 -> 4, of which waited for: 4 -> 4; matrix products, arithmetic and copies ran while one was open for 5% -> 6% of each run, Pallas kernels for 0% -> 0%
where the time goes in v1:
time: 703 us; the launch traced here: 702 us
  waiting for transfers between devices  485 us (69%)
  blocking collectives  115 us (16%)
  matrix products  47.1 us (7%)
  local copies, waits for them, and re-layouts  17.7 us (3%)
  between operations  14.7 us (2%)
  other arithmetic  12.7 us (2%)
  starting transfers between devices  9.92 us (1%)
    reduce_scatter x1, waiting for transfers between devices, local(): lax.psum_scatter(partial_keys.astype(jnp.float32), 'geom', scatter_dimens...  175 us
    reduce_scatter x1, waiting for transfers between devices, local(): lax.psum_scatter(partial_values.astype(jnp.float32), 'geom', scatter_dime...  144 us
    psum x1, blocking collectives, local(): lax.psum((grad_query, grad_key, grad_value, grad_out, grad_up, grad_down,...  115 us
    all_gather x1, waiting for transfers between devices, local(): lax.all_gather(local_values, 'geom', axis=0, tiled=True)  101 us
    all_to_all x1, waiting for transfers between devices, local(): lax.all_to_all(jnp.stack([local_keys] * lax.axis_size('geom')), 'geom', 0...  64.3 us
    unnamed x164, local copies, waits for them, and re-layouts  15.2 us
    dot_general x12, matrix products, mult_nt(): lax.dot_general(left, right, (((1,), (1,)), ((), ())), preferred_element_...  14.9 us
  transfers between devices with their start and end apart: 4, of which 4 were waited for; matrix products, arithmetic and copies ran while one was open for 6% of the time, Pallas kernels for 0%

profile of v1, /device:TPU:0, one launch (start us, length us, event | category | flops | bytes accessed | tf_op | source)
XLA Modules:
  0.0 702.3 jit_solution(1977814720839745133)
XLA Ops:
  7.2 2.1 convolution_convert_fusion.9
  9.3 1.3 convolution_convert_fusion.10
  10.7 2.4 stack.2
  13.1 9.6 %all-to-all-start = ((bf16[32,128,512]{2,1,0:T(8,128)(2,1)}), bf16[32,128,512]{2,1,0:T(8,128)(2,1)}, u32[]{:S(2)}, u32[]{:S(2)}) async-start(bf16[32,128,512]{2,1,0:T(8,128)(2,1)} %stack.2), calls=%async_computation | async-start | bytes 8388608 | tf_op jit(solution)/shard_map/all_to_all | solution.py:151
  23.5 64.3 %all-to-all-done = bf16[32,128,512]{2,1,0:T(8,128)(2,1)} async-done(((bf16[32,128,512]{2,1,0:T(8,128)(2,1)}), bf16[32,128,512]{2,1,0:T(8,128)(2,1)}, u32[]{:S(2)}, u32[]{:S(2)}) %all-to-all-start) | async-done | bytes 4194336 | tf_op jit(solution)/shard_map/all_to_all | solution.py:151
  87.8 1.7 fusion.99
  89.6 1.4 copy-done.8
  90.9 0.4 fusion.5
  91.4 1.7 fusion.98
  93.2 1.3 copy-done.5
  94.4 0.4 fusion.7
  94.9 1.7 fusion.97
  96.7 0.4 fusion.9
  97.1 2.0 fusion.96
  99.2 0.4 fusion.11
  99.6 101.5 %all-gather.2.cloned.1.call-done = bf16[4096,512]{1,0:T(8,128)(2,1)} async-done(((bf16[128,512]{1,0:T(8,128)(2,1)}), bf16[4096,512]{1,0:T(8,128)(2,1)}) %all-gather.2.cloned.1.call-update) | async-done | bytes 4194320 | tf_op jit(solution)/shard_map/all_gather | solution.py:153
  201.1 2.7 convolution_convert_fusion.19
  203.8 1.0 copy-done.76
  204.9 0.7 convolution_convert_fusion.18
  205.6 0.8 copy-done.3
  206.5 0.7 convolution_convert_fusion.17
  207.3 0.7 convolution_convert_fusion.16
  209.3 0.8 copy-done.19
  210.1 0.6 fusion.12
  210.7 1.1 multiply_reduce_fusion.4
  212.4 0.6 convolution_convert_fusion.3
  213.1 0.6 convolution_convert_fusion.2
  213.7 0.6 convolution_convert_fusion.1
  214.4 0.6 convolution_convert_fusion
  215.0 3.6 maximum_convert_fusion.1
  219.3 2.7 multiply_reduce_fusion.3
  222.1 0.7 multiply_convert_fusion.3
  222.9 0.5 convolution_convert_fusion.7
  223.4 0.9 copy-done.77
  224.4 0.9 copy-done.7
  225.2 0.7 multiply_reduce_fusion.2
  225.9 0.7 multiply_convert_fusion.2
  226.7 0.5 convolution_convert_fusion.6
  227.2 1.5 copy-done.4
  228.6 0.7 multiply_reduce_fusion.1
  229.3 0.7 multiply_convert_fusion.1
  230.0 0.5 convolution_convert_fusion.5
  230.8 0.7 multiply_reduce_fusion
  231.4 0.7 multiply_convert_fusion
  232.2 1.0 copy-done.15
  233.1 0.5 convolution_convert_fusion.4
  233.6 3.9 maximum_convert_fusion
  237.5 1.9 convolution_convert_fusion.15
  239.5 1.9 convolution_convert_fusion.14
  241.4 1.8 convolution_convert_fusion.13
  243.2 1.8 convolution_convert_fusion.12
  245.1 0.9 fusion.14
  246.0 0.5 fusion.86
  246.6 1.3 fusion.79
  247.9 1.4 fusion.78
  249.3 1.8 fusion.55
  251.1 1.0 fusion.15
  252.1 144.0 %reduce-scatter.5.cloned.1.call-done = f32[128,512]{1,0:T(8,128)} async-done(((f32[4096,512]{1,0:T(8,128)}), f32[128,512]{1,0:T(8,128)}) %reduce-scatter.5.cloned.1.call-update) | async-done | bytes 262160 | tf_op jit(solution)/shard_map/reduce_scatter | solution.py:170
  396.1 2.6 convolution_bitcast_fusion
  398.7 175.4 %reduce-scatter.3.cloned.1.call-done = f32[128,512]{1,0:T(8,128)} async-done(((f32[4096,512]{1,0:T(8,128)}), f32[128,512]{1,0:T(8,128)}) %reduce-scatter.3.cloned.1.call-update) | async-done | bytes 262160 | tf_op jit(solution)/shard_map/reduce_scatter | solution.py:169
  574.1 2.5 convolution_bitcast_fusion.1
  576.6 115.0 %all-reduce.2 = (bf16[512,512]{1,0:T(8,128)(2,1)}, bf16[512,512]{0,1:T(8,128)(2,1)}, bf16[512,512]{0,1:T(8,128)(2,1)}, bf16[512,512]{1,0:T(8,128)(2,1)}, bf16[51...) all-reduce(f32[512,512]{1,0:T(8,128)} %fusion.78, ...), channel_id=1, replica_groups=mesh['room'=4,'geom'=32] {'room','geom'}, use_global_device_ids=true, to_apply=%region_18.19 | all-reduce | flops 2098176 | bytes 12589056 | tf_op jit(solution)/shard_map/psum | solution.py:190
  691.7 2.0 copy.21
  693.7 2.0 copy.22
  (174 shorter events, 4.0 us)
Async XLA Ops:
  7.2 201.7 %copy-start = (bf16[512,1024]{1,0:T(8,128)(2,1)S(1)}, bf16[512,1024]{1,0:T(8,128)(2,1)}, u32[]{:S(2)}) copy-start(bf16[512,1024]{1,0:T(8,128)(2,1)} %param.20) | copy-start | bytes 3145732
  7.2 193.9 %all-gather.2.cloned.1.call-start = ((), (), s32[]{:S(2)}) async-start(), calls=%async_computation.3 | async-start | bytes 4325376 | tf_op jit(solution)/shard_map/all_gather | solution.py:153
  13.1 9.7 %copy-start.17 = (bf16[1,128,512]{2,1,0:T(8,128)(2,1)S(1)}, bf16[1,128,512]{2,1,0:T(8,128)(2,1)}, u32[]{:S(2)}) copy-start(bf16[1,128,512]{2,1,0:T(8,128)(2,1)} %param.12) | copy-start | bytes 393220
  13.1 10.0 %copy-start.80 = (s32[1,1,32]{2,1,0:T(1,128)S(1)}, s32[1,1,32]{2,1,0:T(1,128)}, u32[]{:S(2)}) copy-start(s32[1,1,32]{2,1,0:T(1,128)} %param.14) | copy-start | bytes 388
  13.1 10.1 %copy-start.28 = (bf16[512,512]{1,0:T(8,128)(2,1)S(1)}, bf16[512,512]{1,0:T(8,128)(2,1)}, u32[]{:S(2)}) copy-start(bf16[512,512]{1,0:T(8,128)(2,1)} %param.16) | copy-start | bytes 1572868
  13.1 10.1 %copy-start.43 = (f32[512]{0:T(512)S(1)}, f32[512]{0:T(512)}, u32[]{:S(2)}) copy-start(f32[512]{0:T(512)} %param.22) | copy-start | bytes 6148
  13.1 74.7 %all-to-all-start = ((bf16[32,128,512]{2,1,0:T(8,128)(2,1)}), bf16[32,128,512]{2,1,0:T(8,128)(2,1)}, u32[]{:S(2)}, u32[]{:S(2)}) async-start(bf16[32,128,512]{2,1,0:T(8,128)(2,1)} %stack.2), calls=%async_computation | async-start | bytes 8388608 | tf_op jit(solution)/shard_map/all_to_all | solution.py:151
  22.7 373.4 %reduce-scatter.5.cloned.1.call-start = ((), (), s32[]{:S(2)}) async-start(), calls=%async_computation.5 | async-start | bytes 8650752 | tf_op jit(solution)/shard_map/reduce_scatter | solution.py:170
  22.9 68.5 %copy-start.45 = (f32[128]{0:T(128)}, f32[128]{0:T(128)S(1)}, u32[]{:S(2)}) copy-start(f32[128]{0:T(128)S(1)} %broadcast_multiply_fusion.3) | copy-start | bytes 1540
  23.1 68.2 %copy-start.60 = (f32[128]{0:T(128)}, f32[128]{0:T(128)S(1)}, u32[]{:S(2)}) copy-start(f32[128]{0:T(128)S(1)} %add_rsqrt_fusion.1) | copy-start | bytes 1540
  23.5 73.6 %copy-start.22 = (bf16[128,512]{1,0:T(8,128)(2,1)}, bf16[128,512]{1,0:T(8,128)(2,1)S(1)}, u32[]{:S(2)}) copy-start(bf16[128,512]{1,0:T(8,128)(2,1)S(1)} %convolution_convert_fusion.11) | copy-start | bytes 393220
  89.6 111.5 %copy-start.56 = (f32[128]{0:T(128)}, f32[128]{0:T(128)S(1)}, u32[]{:S(2)}) copy-start(f32[128]{0:T(128)S(1)} %get-tuple-element.35) | copy-start | bytes 1540
  91.4 109.7 %copy-start.71 = (f32[128]{0:T(128)}, f32[128]{0:T(128)S(1)}, u32[]{:S(2)}) copy-start(f32[128]{0:T(128)S(1)} %fusion.5) | copy-start | bytes 1540
  93.1 110.7 %copy-start.53 = (f32[128]{0:T(128)}, f32[128]{0:T(128)S(1)}, u32[]{:S(2)}) copy-start(f32[128]{0:T(128)S(1)} %get-tuple-element.33) | copy-start | bytes 1540
  94.9 108.9 %copy-start.68 = (f32[128]{0:T(128)}, f32[128]{0:T(128)S(1)}, u32[]{:S(2)}) copy-start(f32[128]{0:T(128)S(1)} %fusion.7) | copy-start | bytes 1540
  96.6 2.5 copy-start.2
  96.6 109.0 %copy-start.50 = (f32[128]{0:T(128)}, f32[128]{0:T(128)S(1)}, u32[]{:S(2)}) copy-start(f32[128]{0:T(128)S(1)} %get-tuple-element.31) | copy-start | bytes 1540
  97.1 108.5 %copy-start.65 = (f32[128]{0:T(128)}, f32[128]{0:T(128)S(1)}, u32[]{:S(2)}) copy-start(f32[128]{0:T(128)S(1)} %fusion.9) | copy-start | bytes 1540
  99.1 108.1 %copy-start.47 = (f32[128]{0:T(128)}, f32[128]{0:T(128)S(1)}, u32[]{:S(2)}) copy-start(f32[128]{0:T(128)S(1)} %get-tuple-element.29) | copy-start | bytes 1540
  99.6 107.6 %copy-start.62 = (f32[128]{0:T(128)}, f32[128]{0:T(128)S(1)}, u32[]{:S(2)}) copy-start(f32[128]{0:T(128)S(1)} %fusion.11) | copy-start | bytes 1540
  201.1 2.7 copy-start.6
  201.1 3.8 copy-start.76
  204.9 3.1 copy-start.34
  204.9 1.6 copy-start.3
  206.5 1.5 copy-start.36
  207.3 1.7 copy-start.42
  208.3 1.8 copy-start.30
  208.3 1.8 copy-start.78
  210.7 1.7 copy-start.9
  210.7 1.7 copy-start.57
  210.7 1.7 copy-start.72
  212.4 2.0 copy-start.32
  218.6 355.5 %reduce-scatter.3.cloned.1.call-start = ((), (), s32[]{:S(2)}) async-start(), calls=%async_computation.4 | async-start | bytes 8650752 | tf_op jit(solution)/shard_map/reduce_scatter | solution.py:169
  219.3 2.7 copy-start.10
  219.3 2.7 copy-start.59
  219.3 2.7 copy-start.74
  222.0 2.3 copy-start.77
  222.9 2.3 copy-start.7
  222.9 2.3 copy-start.55
  222.9 2.3 copy-start.70
  226.6 2.7 copy-start.11
  226.6 2.0 copy-start.4
  226.6 2.0 copy-start.52
  226.7 2.0 copy-start.67
  230.0 1.4 copy-start.13
  237.5 1.9 copy-start.12
  237.5 3.8 copy-start.14
  239.5 3.8 copy-start.16
  241.3 3.7 copy-start.29
  241.4 3.7 copy-start.46
  241.4 3.7 copy-start.61
  243.2 2.8 copy-start.27
  245.1 1.5 copy-start.25
  245.1 1.5 copy-start.35
  245.1 1.5 copy-start.37
  245.1 1.5 copy-start.39
  245.1 1.5 copy-start.41
  246.0 3.3 copy-start.20
  246.0 3.3 copy-start.31
  247.9 3.3 copy-start.79
  249.3 146.8 %copy-start.21 = (bf16[1,128,512]{2,1,0:T(8,128)(2,1)S(1)}, bf16[1,128,512]{2,1,0:T(8,128)(2,1)}, u32[]{:S(2)}) copy-start(bf16[1,128,512]{2,1,0:T(8,128)(2,1)} %param.13) | copy-start | bytes 393220
  251.1 325.5 %copy-start.44 = (f32[512]{0:T(512)S(1)}, f32[512]{0:T(512)}, u32[]{:S(2)}) copy-start(f32[512]{0:T(512)} %get-tuple-element.18) | copy-start | bytes 6148
  251.1 325.5 %copy-start.75 = (f32[512]{0:T(512)S(1)}, f32[512]{0:T(512)}, u32[]{:S(2)}) copy-start(f32[512]{0:T(512)} %fusion.14) | copy-start | bytes 6148
  576.6 119.1 %copy-start.1 = (bf16[512,1024]{1,0:T(8,128)(2,1)S(1)}, bf16[512,1024]{1,0:T(8,128)(2,1)}, u32[]{:S(2)}) copy-start(bf16[512,1024]{1,0:T(8,128)(2,1)} %param.20) | copy-start | bytes 3145732
  (21 other events, 18.2 us)
Sparse Core Ops, SparseCore 0:
  10.2 190.7 all-gather.1
  218.7 177.3 reduce-scatter.4
  398.5 175.5 reduce-scatter.2
